TPU v7x, 256 devices: a whole 4x4x8 slice. The times are simulated.
256 devices in a mesh: ctx: 64 (over x_hi, z, y), head: 4 (over x_lo, core).
Axes of the slice: x: 4 (x_hi: 2, x_lo: 2; x = x_hi * 2 + x_lo), y: 4, z: 8, core: 2. Of those that a mesh axis runs over, the one named last changes fastest.
Arguments:
- queries: bfloat16 [8192, 4096], P('ctx', 'head'), may hold values from -81 to 81
- key_states: bfloat16 [8192, 1024], P('ctx', 'head'), may hold values from -7 to 7
- value_states: bfloat16 [8192, 1024], P('ctx', 'head'), may hold values from -6 to 6
- out_weight: bfloat16 [4096, 4096], P('head'), may hold values from -0.09375 to 0.09375
- head_role: int32 [8], replicated, may hold values from 0 to 1, as said below
- sink_len: int32 [8], replicated, may hold values from 32 to 128, as said below
- window_len: int32 [8], replicated, may hold values from 256 to 1024, as said below
Outputs:
- mixed: bfloat16 [8192, 4096], P(('ctx', 'head'))
Inputs may be any that keep to these rules, and one draw needn't show every extreme that they name: `head_role`: exactly 4 heads are retrieval heads. `sink_len`: some head has exactly 128. `window_len`: some head has exactly 1024.
All inputs are finite; a program needn't handle non-finite values.
Results may differ from a plain program's by a relative error of at most 0.012.
Values may be sent and summed in bfloat16 or wider, within the bound.
A program may use at most 128 MiB of HBM per device.

v0:
```python
import jax
import jax.numpy as jnp
from jax import lax
from jax.sharding import PartitionSpec as P

HD = 128
GROUP = 4
NEGATIVE = -1e30


def online_update(running, query_heads, key_part, value_part, allowed):
    row_peak, row_total, weighted = running
    scores = jnp.einsum(
        "thgd,jhd->thgj", query_heads, key_part, preferred_element_type=jnp.float32
    ) * HD ** (-0.5)
    visible = allowed[:, :, None, :]
    block_peak = jnp.max(jnp.where(visible, scores, NEGATIVE), axis=-1)
    new_peak = jnp.maximum(row_peak, block_peak)
    weights = jnp.where(visible, jnp.exp(scores - new_peak[..., None]), 0.0)
    row_total = jnp.sum(weights, axis=-1)
    weighted = jnp.einsum(
        "thgj,jhd->thgd",
        weights.astype(jnp.bfloat16),
        value_part,
        preferred_element_type=jnp.float32,
    )
    return (new_peak, row_total, weighted)


def empty_state(row_count, head_count):
    return (
        jnp.full((row_count, head_count, GROUP), NEGATIVE, jnp.float32),
        jnp.zeros((row_count, head_count, GROUP), jnp.float32),
        jnp.zeros((row_count, head_count, GROUP, HD), jnp.float32),
    )


def finish(running, row_count):
    row_peak, row_total, weighted = running
    return (weighted / row_total[..., None]).astype(jnp.bfloat16).reshape(row_count, -1)


def per_device(queries, key_states, value_states, out_weight, head_role, sink_len, window_len):
    row_count = queries.shape[0]
    local_heads = key_states.shape[1] // HD
    row_base = lax.axis_index("ctx") * row_count
    query_pos = row_base + jnp.arange(row_count, dtype=jnp.int32)
    my_group = lax.axis_index("head")
    first_head = my_group * local_heads
    last_row = row_base + row_count - 1
    roles_here = lax.dynamic_slice_in_dim(head_role, first_head, local_heads)
    sinks_here = lax.dynamic_slice_in_dim(sink_len, first_head, local_heads)
    windows_here = lax.dynamic_slice_in_dim(window_len, first_head, local_heads)
    query_heads = queries.reshape(row_count, local_heads, GROUP, HD)
    width = key_states.shape[1]
    both = lax.all_gather(
        jnp.concatenate([key_states, value_states], axis=1), "ctx", axis=0, tiled=True
    )
    key_part = both[:, :width].reshape(-1, local_heads, HD)
    value_part = both[:, width:].reshape(-1, local_heads, HD)
    key_pos = jnp.arange(key_part.shape[0], dtype=jnp.int32)

    def update(state):
        later = query_pos[:, None, None]
        earlier = key_pos[None, None, :]
        allowed = (earlier <= later) & (
            (roles_here[None, :, None] == 1)
            | (earlier < sinks_here[None, :, None])
            | (later - earlier < windows_here[None, :, None])
        )
        return online_update(state, query_heads, key_part, value_part, allowed)

    def unchanged(state):
        return state

    running = lax.cond(
        jnp.int32(0) <= last_row, update, unchanged, empty_state(row_count, local_heads)
    )
    attended = finish(running, row_count)
    mixed = lax.psum_scatter(
        jnp.dot(attended, out_weight, preferred_element_type=jnp.float32).astype(jnp.bfloat16),
        "head",
        scatter_dimension=0,
        tiled=True,
    )
    return mixed


def solution(mesh):
    in_specs = (
        P("ctx", "head"),
        P("ctx", "head"),
        P("ctx", "head"),
        P("head", None),
        P(),
        P(),
        P(),
    )
    out_specs = P(("ctx", "head"), None)
    return jax.shard_map(
        per_device, mesh=mesh, in_specs=in_specs, out_specs=out_specs, check_vma=False
    )
```

profile of v0, /device:TPU:1, one launch (start us, length us, event | category | flops | bytes accessed | tf_op | source)
XLA Modules:
  0.0 275.3 jit_solution(8369988572290120255)
XLA Ops:
  6.5 0.0 all-gather.2.cloned.1.call-start
  6.5 0.9 copy.27
  7.5 1.0 copy.28
  8.5 0.7 pad_maximum_fusion
  9.1 0.0 all-gather.2.cloned.1.call-update
  9.1 0.0 reduce-scatter.2.cloned.1.call-start
  9.2 173.6 %all-gather.2.cloned.1.call-done = bf16[8192,512]{0,1:T(8,128)(2,1)} async-done(((bf16[128,512]{0,1:T(8,128)(2,1)}), bf16[8192,512]{0,1:T(8,128)(2,1)}) %all-gather.2.cloned.1.call-update) | async-done | bytes 8388624 | tf_op jit(solution)/shard_map/all_gather | solution.py:56
  182.8 57.6 %conditional.1 = (f32[128,2,4]{0,2,1:T(4,128)S(1)}, f32[128,2,4,128]{0,3,2,1:T(8,128)S(1)}) conditional(s32[]{:T(128)} %convert_element_type.15, () %tuple.22, (s32[8192]{0:T(1024)S(1)}, s32[8192]{0:T(1024)S(1)}, s32[]{:T(128)}, s32[128]{0:T(128)S(1)}, s32[]{:T(128)}, /*index=5*/s32[8]{0:T(128)}, s32[8192]{0:T(1024)S(1)}, s32[8]{0:T(128)}, ...), branch_computations={%region_0.0_spmd, %region_1.4_spmd} | conditional | flops 4395662336 | bytes 180775088 | solution.py:76
  182.8 0.7 dynamic-slice_compare_fusion
  183.6 0.7 dynamic_slice.19
  184.3 0.7 dynamic_slice.20
  185.0 0.1 compare_or_fusion
  185.1 1.1 reshape.126
  186.2 0.0 copy-start
  186.3 3.7 %broadcast_compare_fusion = pred[128,8192]{0,1:T(8,128)(4,1)S(1)} fusion(s32[128]{0:T(128)S(1)} %broadcast_add_fusion, s32[8192]{0:T(1024)S(1)} %get-tuple-element.122), kind=kLoop, calls=%fused_computation.11 | loop fusion | flops 1048576 | bytes 1081856 | tf_op jit(solution)/shard_map/cond/branch_1_fun/le | solution.py:66
  190.0 1.2 broadcast_subtract_fusion
  191.2 2.8 %or_and_fusion = pred[128,2,8192]{0,2,1:T(8,128)(4,1)S(1)} fusion(s32[128,8192]{0,1:T(8,128)S(1)} %broadcast_subtract_fusion, s32[2]{0:T(128)S(1)} %dynamic_slice.20, pred[2,8192]{1,0:T(4,128)(4,1)S(1)} %compare_or_fusion, pred[128,8192]{0,1:T(8,128)(4,1)S(1)} %broadcast_compare_fusion), kind=kLoop, calls=%fused_computation.9 | loop fusion | flops 6291456 | bytes 7356424 | tf_op jit(solution)/shard_map/cond/branch_1_fun/and | solution.py:66
  194.0 0.0 copy-done
  194.1 2.3 fusion.15
  196.3 13.6 %fusion = (f32[128,2,4]{0,2,1:T(4,128)S(1)}, f32[2,8192,128,4]{2,1,3,0:T(8,128)}) fusion(pred[128,2,8192]{0,2,1:T(8,128)(4,1)S(1)} %or_and_fusion, bf16[8192,2,128,1]{0,2,3,1:T(8,128)(2,1)S(1)} %bitcast.33, bf16[128,2,4,128]{3,2,1,0:T(4,128)(2,1)S(1)} %reshape.126), kind=kOutput, calls=%fused_computation.2 | convolution fusion | flops 2172648448 | bytes 40112128 | tf_op jit(solution)/shard_map/cond/branch_1_fun/thgd,jhd->thgj/dot_general | solution.py:13
  209.9 15.9 %fusion.8 = f32[128,2,4,128]{3,0,2,1:T(8,128)S(1)} fusion(bf16[8192,2,128,1]{0,2,3,1:T(8,128)(2,1)} %bitcast.34, f32[2,8192,128,4]{2,1,3,0:T(8,128)} %get-tuple-element.144, f32[128,2,4]{0,2,1:T(4,128)S(1)} %broadcast_maximum_fusion, pred[128,2,8192]{0,2,1:T(8,128)(4,1)S(1)} %or_and_fusion), kind=kOutput, calls=%fused_computation.12 | convolution fusion | flops 2181038080 | bytes 40374272 | tf_op jit(solution)/shard_map/cond/branch_1_fun/thgj,jhd->thgd/dot_general | solution.py:21
  225.8 14.4 %fusion.4 = f32[128,2,4]{0,2,1:T(4,128)S(1)} fusion(f32[2,8192,128,4]{2,1,3,0:T(8,128)} %get-tuple-element.144, f32[128,2,4]{0,2,1:T(4,128)S(1)} %broadcast_maximum_fusion, pred[128,2,8192]{0,2,1:T(8,128)(4,1)S(1)} %or_and_fusion), kind=kLoop, calls=%fused_computation.6 | loop fusion | flops 33553408 | bytes 35659776 | tf_op jit(solution)/shard_map/cond/branch_1_fun/reduce_sum | solution.py:20
  240.2 0.2 copy.38
  240.4 0.1 divide_convert_fusion
  240.4 5.7 %convolution_convert_fusion = bf16[128,4096]{1,0:T(8,128)(2,1)} fusion(bf16[128,1024]{0,1:T(8,128)(2,1)S(1)} %bitcast.35, bf16[1024,4096]{1,0:T(8,128)(2,1)} %param.12), kind=kOutput, calls=%fused_computation.21 | convolution fusion | flops 1074266112 | bytes 9699328 | tf_op jit(solution)/shard_map/dot_general | solution.py:81
  246.1 0.0 reduce-scatter.2.cloned.1.call-update
  246.1 22.3 %reduce-scatter.2.cloned.1.call-done = bf16[32,4096]{1,0:T(8,128)(2,1)} async-done(((bf16[128,4096]{1,0:T(8,128)(2,1)}), bf16[32,4096]{1,0:T(8,128)(2,1)}) %reduce-scatter.2.cloned.1.call-update) | async-done | bytes 262160 | tf_op jit(solution)/shard_map/reduce_scatter | solution.py:80
  (4 shorter events, 0.0 us)
Async XLA Ops:
  6.5 176.3 %all-gather.2.cloned.1.call-start = ((), (), s32[]{:S(2)}) async-start(), calls=%async_computation.1 | async-start | bytes 8519680 | tf_op jit(solution)/shard_map/all_gather | solution.py:56
  9.1 259.3 %reduce-scatter.2.cloned.1.call-start = ((), (), s32[]{:S(2)}) async-start(), calls=%async_computation.2 | async-start | bytes 1310720 | tf_op jit(solution)/shard_map/reduce_scatter | solution.py:80
  186.2 7.8 %copy-start = (bf16[8192,512]{0,1:T(8,128)(2,1)S(1)}, bf16[8192,512]{0,1:T(8,128)(2,1)}, u32[]{:S(2)}) copy-start(bf16[8192,512]{0,1:T(8,128)(2,1)} %get-tuple-element.126) | copy-start | bytes 25165828 | tf_op jit(solution)/shard_map/cond
Sparse Core Ops, SparseCore 0:
  10.8 171.9 all-gather.1
  246.2 22.1 reduce-scatter.1
where the time goes:
time: 276 us; the launch traced here: 275 us
  waiting for transfers between devices  196 us (71%)
  matrix products  35.1 us (13%)
  other arithmetic  23.7 us (9%)
  between operations  13.4 us (5%)
  local copies, waits for them, and re-layouts  6.97 us (3%)
    all_gather x1, waiting for transfers between devices, per_device(): lax.all_gather(jnp.concatenate([key_states, value_states], axis=1), 'ctx'...  174 us
    reduce_scatter x1, waiting for transfers between devices, per_device(): lax.psum_scatter(jnp.dot(attended, out_weight, preferred_element_type=jnp...  22.3 us
    dot_general x1, matrix products, online_update(): jnp.einsum('thgj,jhd->thgd', weights.astype(jnp.bfloat16), value_part, pr...  15.9 us
    reduce_sum x1, other arithmetic, online_update(): row_total = jnp.sum(weights, axis=-1)  14.4 us
    dot_general x1, matrix products, online_update(): jnp.einsum('thgd,jhd->thgj', query_heads, key_part, preferred_element_typ...  13.6 us
    dot_general x1, matrix products, per_device(): jnp.dot(attended, out_weight, preferred_element_type=jnp.float32)  5.65 us
  transfers between devices with their start and end apart: 2, of which 2 were waited for; matrix products, arithmetic and copies ran while one was open for 0% of the time, Pallas kernels for 0%

commit v1 on v0

--- a/solution.py
+++ b/solution.py
@@ -53,8 +53,14 @@
     windows_here = lax.dynamic_slice_in_dim(window_len, first_head, local_heads)
     query_heads = queries.reshape(row_count, local_heads, GROUP, HD)
     width = key_states.shape[1]
-    both = lax.all_gather(
-        jnp.concatenate([key_states, value_states], axis=1), "ctx", axis=0, tiled=True
+    both = jnp.concatenate(
+        lax.all_to_all(
+            jnp.stack([jnp.concatenate([key_states, value_states], axis=1)] * lax.axis_size("ctx")),
+            "ctx",
+            0,
+            0,
+        ),
+        axis=0,
     )
     key_part = both[:, :width].reshape(-1, local_heads, HD)
     value_part = both[:, width:].reshape(-1, local_heads, HD)

time: 276 us -> 314 us (1.14)
  starting transfers between devices: 0.04 us -> 15.7 us
  local copies, waits for them, and re-layouts: 6.97 us -> 19.6 us
  waiting for transfers between devices: 196 us -> 205 us
    all_to_all x0 -> x1, waiting for transfers between devices: none -> 183 us  [per_device(): lax.all_to_all(jnp.stack([jnp.concatenate([key_states, value_states], axi...]
    all_gather x1 -> x0, waiting for transfers between devices: 174 us -> none  [per_device(): lax.all_gather(jnp.concatenate([key_states, value_states], axis=1), 'ctx'...]
    all_to_all x0 -> x1, starting transfers between devices: none -> 15.5 us  [per_device(): lax.all_to_all(jnp.stack([jnp.concatenate([key_states, value_states], axi...]
    reshape x0 -> x1, local copies, waits for them, and re-layouts: none -> 7.84 us  [per_device(): jnp.concatenate(lax.all_to_all(jnp.stack([jnp.concatenate([key_states, va...]
    another operation x0 -> x1, local copies, waits for them, and re-layouts: none -> 5.25 us  [per_device(): jnp.stack([jnp.concatenate([key_states, value_states], axis=1)] * lax.axi...]
where the time goes in v1:
time: 314 us
  waiting for transfers between devices  205 us (65%)
  matrix products  35.1 us (11%)
  other arithmetic  24.3 us (8%)
  local copies, waits for them, and re-layouts  19.6 us (6%)
  starting transfers between devices  15.7 us (5%)
  between operations  13.5 us (4%)
    all_to_all x1, waiting for transfers between devices, per_device(): lax.all_to_all(jnp.stack([jnp.concatenate([key_states, value_states], axi...  183 us
    reduce_scatter x1, waiting for transfers between devices, per_device(): lax.psum_scatter(jnp.dot(attended, out_weight, preferred_element_type=jnp...  22.8 us
    dot_general x1, matrix products, online_update(): jnp.einsum('thgj,jhd->thgd', weights.astype(jnp.bfloat16), value_part, pr...  15.9 us
    all_to_all x1, starting transfers between devices, per_device(): lax.all_to_all(jnp.stack([jnp.concatenate([key_states, value_states], axi...  15.5 us
    reduce_sum x1, other arithmetic, online_update(): row_total = jnp.sum(weights, axis=-1)  14.4 us
    dot_general x1, matrix products, online_update(): jnp.einsum('thgd,jhd->thgj', query_heads, key_part, preferred_element_typ...  13.5 us
    reshape x1, local copies, waits for them, and re-layouts, per_device(): jnp.concatenate(lax.all_to_all(jnp.stack([jnp.concatenate([key_states, va...  7.84 us
  transfers between devices with their start and end apart: 2, of which 2 were waited for; matrix products, arithmetic and copies ran while one was open for 0% of the time, Pallas kernels for 0%

profile of v1, /device:TPU:1, one launch (start us, length us, event | category | flops | bytes accessed | tf_op | source)
XLA Modules:
  0.0 313.7 jit_solution(2997313566743088059)
XLA Ops:
  6.5 0.9 pad_maximum_fusion
  7.4 0.1 copy.26
  7.5 5.2 %stack.2 = bf16[64,128,512]{1,2,0:T(8,128)(2,1)} broadcast(bf16[128,512]{0,1:T(8,128)(2,1)S(1)} %copy.26), dimensions={1,2} | broadcast | bytes 8519680 | tf_op jit(solution)/shard_map/stack | solution.py:58
  12.8 0.0 copy-start
  12.8 0.0 copy-start.1
  12.8 0.0 copy-start.2
  12.8 0.0 copy-start.3
  12.8 15.5 %all-to-all-start = ((bf16[64,128,512]{1,2,0:T(8,128)(2,1)}), bf16[64,128,512]{1,2,0:T(8,128)(2,1)}, u32[]{:S(2)}, u32[]{:S(2)}) async-start(bf16[64,128,512]{1,2,0:T(8,128)(2,1)} %stack.2), calls=%async_computation | async-start | bytes 16777216 | tf_op jit(solution)/shard_map/all_to_all | solution.py:57
  28.3 0.2 reduce-scatter.2.cloned.1.call-start
  28.6 182.6 %all-to-all-done = bf16[64,128,512]{1,2,0:T(8,128)(2,1)} async-done(((bf16[64,128,512]{1,2,0:T(8,128)(2,1)}), bf16[64,128,512]{1,2,0:T(8,128)(2,1)}, u32[]{:S(2)}, u32[]{:S(2)}) %all-to-all-start) | async-done | bytes 8388640 | tf_op jit(solution)/shard_map/all_to_all | solution.py:57
  211.1 0.0 copy-done
  211.1 0.0 copy-done.1
  211.2 0.0 copy-done.2
  211.2 0.0 copy-done.3
  211.2 66.1 %conditional.1 = (f32[128,2,4]{0,2,1:T(4,128)S(1)}, f32[128,2,4,128]{0,3,2,1:T(8,128)}) conditional(s32[]{:T(128)} %convert_element_type.15, () %tuple.23, (s32[8192]{0:T(1024)S(1)}, s32[8192]{0:T(1024)S(1)}, s32[]{:T(128)}, s32[128]{0:T(128)S(1)}, s32[]{:T(128)}, /*index=5*/s32[8]{0:T(128)S(1)}, s32[8192]{0:T(1024)S(1)}, s32[8]{0:T(128)S(1)}, ...), branch_computations={%region_0.0_spmd, %region_1.4_spmd} | conditional | flops 4395662336 | bytes 163997840 | solution.py:82
  211.2 0.1 dynamic_slice.20
  211.3 0.1 dynamic_slice.19
  211.4 0.1 dynamic-slice_compare_fusion
  211.4 0.1 compare_or_fusion
  211.6 0.2 reshape.134
  211.7 3.7 %broadcast_compare_fusion = pred[128,8192]{0,1:T(8,128)(4,1)S(1)} fusion(s32[128]{0:T(128)S(1)} %broadcast_add_fusion, s32[8192]{0:T(1024)S(1)} %get-tuple-element.119), kind=kLoop, calls=%fused_computation.12 | loop fusion | flops 1048576 | bytes 1081856 | tf_op jit(solution)/shard_map/cond/branch_1_fun/le | solution.py:72
  215.5 1.2 broadcast_subtract_fusion
  216.7 2.8 or_and_fusion
  219.5 7.8 %copy_bitcast_fusion = bf16[8192,512]{0,1:T(8,128)(2,1)} fusion(bf16[64,128,512]{1,2,0:T(8,128)(2,1)} %get-tuple-element.146), kind=kLoop, calls=%fused_computation.9 | loop fusion | bytes 16777216 | tf_op jit(solution)/shard_map/reshape | solution.py:56
  227.4 5.1 %fusion.15 = (bf16[8192,256]{0,1:T(8,128)(2,1)}, bf16[8192,256]{0,1:T(8,128)(2,1)S(1)}) fusion(bf16[8192,512]{0,1:T(8,128)(2,1)} %copy_bitcast_fusion), kind=kLoop, calls=%fused_computation.25 | loop fusion | bytes 16777216 | tf_op jit(solution)/shard_map/slice | solution.py:66
  232.4 13.5 %fusion = (f32[128,2,4]{0,2,1:T(4,128)S(1)}, f32[2,8192,128,4]{2,1,3,0:T(8,128)}) fusion(pred[128,2,8192]{0,2,1:T(8,128)(4,1)S(1)} %or_and_fusion, bf16[8192,2,128,1]{0,2,3,1:T(8,128)(2,1)S(1)} %bitcast.38, bf16[128,2,4,128]{3,2,1,0:T(4,128)(2,1)S(1)} %reshape.134), kind=kOutput, calls=%fused_computation.2 | convolution fusion | flops 2172648448 | bytes 40112128 | tf_op jit(solution)/shard_map/cond/branch_1_fun/thgd,jhd->thgj/dot_general | solution.py:13
  246.0 15.9 %fusion.8 = f32[128,2,4,128]{3,0,2,1:T(8,128)S(1)} fusion(bf16[8192,2,128,1]{0,2,3,1:T(8,128)(2,1)} %bitcast.39, f32[2,8192,128,4]{2,1,3,0:T(8,128)} %get-tuple-element.152, f32[128,2,4]{0,2,1:T(4,128)S(1)} %broadcast_maximum_fusion, pred[128,2,8192]{0,2,1:T(8,128)(4,1)S(1)} %or_and_fusion), kind=kOutput, calls=%fused_computation.13 | convolution fusion | flops 2181038080 | bytes 40374272 | tf_op jit(solution)/shard_map/cond/branch_1_fun/thgj,jhd->thgd/dot_general | solution.py:21
  261.9 14.4 %fusion.4 = f32[128,2,4]{0,2,1:T(4,128)S(1)} fusion(f32[2,8192,128,4]{2,1,3,0:T(8,128)} %get-tuple-element.152, f32[128,2,4]{0,2,1:T(4,128)S(1)} %broadcast_maximum_fusion, pred[128,2,8192]{0,2,1:T(8,128)(4,1)S(1)} %or_and_fusion), kind=kLoop, calls=%fused_computation.6 | loop fusion | flops 33553408 | bytes 35659776 | tf_op jit(solution)/shard_map/cond/branch_1_fun/reduce_sum | solution.py:20
  276.3 1.0 copy.37
  277.3 1.1 divide_convert_fusion
  278.4 5.6 %convolution_convert_fusion = bf16[128,4096]{1,0:T(8,128)(2,1)} fusion(bf16[128,1024]{0,1:T(8,128)(2,1)S(1)} %bitcast.40, bf16[1024,4096]{1,0:T(8,128)(2,1)} %param.12), kind=kOutput, calls=%fused_computation.22 | convolution fusion | flops 1074266112 | bytes 9699328 | tf_op jit(solution)/shard_map/dot_general | solution.py:87
  284.0 0.0 reduce-scatter.2.cloned.1.call-update
  284.0 22.8 %reduce-scatter.2.cloned.1.call-done = bf16[32,4096]{1,0:T(8,128)(2,1)} async-done(((bf16[128,4096]{1,0:T(8,128)(2,1)}), bf16[32,4096]{1,0:T(8,128)(2,1)}) %reduce-scatter.2.cloned.1.call-update) | async-done | bytes 262160 | tf_op jit(solution)/shard_map/reduce_scatter | solution.py:86
  (4 shorter events, 0.0 us)
Async XLA Ops:
  12.8 198.4 %copy-start = (bf16[128,1024]{1,0:T(8,128)(2,1)S(1)}, bf16[128,1024]{1,0:T(8,128)(2,1)}, u32[]{:S(2)}) copy-start(bf16[128,1024]{1,0:T(8,128)(2,1)} %param.9) | copy-start | bytes 786436
  12.8 198.4 %copy-start.1 = (s32[8]{0:T(128)S(1)}, s32[8]{0:T(128)}, u32[]{:S(2)}) copy-start(s32[8]{0:T(128)} %param.13) | copy-start | bytes 100
  12.8 198.4 %copy-start.2 = (s32[8]{0:T(128)S(1)}, s32[8]{0:T(128)}, u32[]{:S(2)}) copy-start(s32[8]{0:T(128)} %param.14) | copy-start | bytes 100
  12.8 198.4 %copy-start.3 = (s32[8]{0:T(128)S(1)}, s32[8]{0:T(128)}, u32[]{:S(2)}) copy-start(s32[8]{0:T(128)} %param.15) | copy-start | bytes 100
  12.8 198.3 %all-to-all-start = ((bf16[64,128,512]{1,2,0:T(8,128)(2,1)}), bf16[64,128,512]{1,2,0:T(8,128)(2,1)}, u32[]{:S(2)}, u32[]{:S(2)}) async-start(bf16[64,128,512]{1,2,0:T(8,128)(2,1)} %stack.2), calls=%async_computation | async-start | bytes 16777216 | tf_op jit(solution)/shard_map/all_to_all | solution.py:57
  28.3 278.5 %reduce-scatter.2.cloned.1.call-start = ((), (), s32[]{:S(2)}) async-start(), calls=%async_computation.2 | async-start | bytes 1310720 | tf_op jit(solution)/shard_map/reduce_scatter | solution.py:86
Sparse Core Ops, SparseCore 0:
  284.2 22.6 reduce-scatter.1
